TPU v7x, 256 devices: a whole 4x4x8 slice. The times are simulated.
256 devices in a mesh: freq: 8 (over z), lat: 8 (over x, y_hi), lon: 4 (over y_lo, core).
Axes of the slice: x: 4, y: 4 (y_hi: 2, y_lo: 2; y = y_hi * 2 + y_lo), z: 8, core: 2. Of those that a mesh axis runs over, the one named last changes fastest.
Arguments:
- direction: float32 [3, 32, 1024, 2048], P(None, 'freq', 'lat', 'lon'), may hold values from -6 to 6
- base_flow: float32 [2, 32, 1024, 2048], P(None, 'freq', 'lat', 'lon'), may hold values from -2 to 2
- water_depth: float32 [1024, 2048], P('lat', 'lon'), may hold values from 0.5 to 2
- drag_factor: float32 [1024, 2048], P('lat', 'lon'), may hold values from 0.2 to 2
- wet_mask: int32 [1024, 2048], P('lat', 'lon'), may hold values 0 or 1
Outputs:
- result: float32 [3, 32, 1024, 2048], P(None, 'freq', 'lat', 'lon')
All inputs are finite; a program needn't handle non-finite values. No bound on the sum of `wet_mask` on one device may be relied on, other than what follows from the above.
Results may differ from a plain program's by a relative error of at most 0.000071.
Values sent between devices are 32-bit elements; how exact they have to be, the bound alone decides.
A program may use at most 128 MiB of HBM per device.

v0:
```python
import math

import jax
import jax.numpy as jnp
from jax import lax
from jax.sharding import PartitionSpec as P

NCON = 16
NTIME = 256


LINEAR_DRAG = 0.5
GRAVITY = 1.0
OMEGA_STEP = 0.25
SPEED_SOFT = 0.01


def extended_2(block, sides, width):
    for axis, dim in sides:
        count = lax.axis_size(axis)
        forward = [(i, i + 1) for i in range(count - 1)]
        forward.append((count - 1, 0))
        backward = [(target, source) for source, target in forward]
        low = lax.ppermute(
            lax.slice_in_dim(block, block.shape[dim] - width, None, axis=dim), axis, forward
        )
        high = lax.ppermute(lax.slice_in_dim(block, 0, width, axis=dim), axis, backward)
        block = jnp.concatenate([low, block, high], axis=dim)
    return block


def samples_table(sample_count, constituents):
    sample_index = jnp.arange(sample_count, dtype=jnp.int32)
    harmonic = jnp.arange(1, constituents + 1, dtype=jnp.int32)
    wrapped_turns = sample_index[:, None] * harmonic[None, :] % sample_count
    phase_angle = wrapped_turns.astype(jnp.float32) * (2.0 * math.pi / sample_count)
    table = jnp.stack([jnp.cos(phase_angle), jnp.sin(phase_angle)], axis=2)
    return table.reshape(sample_count, 2 * constituents)


def rotation_of(row_index, total_rows):
    return 0.5 + (row_index.astype(jnp.float32) + 0.5) / total_rows


def tendency(values, angular):
    cos_sin = values.reshape((values.shape[0] // 2, 2) + values.shape[1:])
    moved = jnp.stack([angular * cos_sin[:, 1], -angular * cos_sin[:, 0]], axis=1)
    return moved.reshape(values.shape)


def linear_residual(extended, tile_rows, tile_cols, angular, rotation):

    def neighbour(plane, row_step, col_step):
        return extended[
            plane,
            :,
            1 + row_step : 1 + row_step + tile_rows,
            1 + col_step : 1 + col_step + tile_cols,
        ]

    height = neighbour(0, 0, 0)
    east = neighbour(1, 0, 0)
    north = neighbour(2, 0, 0)
    res_height = (
        tendency(height, angular)
        + neighbour(3, 0, 0)
        - neighbour(3, 0, -1)
        + neighbour(4, 0, 0)
        - neighbour(4, -1, 0)
    )
    north_mean = 0.25 * (north + neighbour(2, 0, 1) + neighbour(2, -1, 0) + neighbour(2, -1, 1))
    east_mean = 0.25 * (east + neighbour(1, 0, -1) + neighbour(1, 1, 0) + neighbour(1, 1, -1))
    res_east = (
        tendency(east, angular)
        + LINEAR_DRAG * east
        - rotation * north_mean
        + GRAVITY * (neighbour(0, 0, 1) - height)
    )
    res_north = (
        tendency(north, angular)
        + LINEAR_DRAG * north
        + rotation * east_mean
        + GRAVITY * (neighbour(0, 1, 0) - height)
    )
    return jnp.stack([res_height, res_east, res_north])


def friction_row(row_block, drag_row, table):
    highest = lax.Precision.HIGHEST
    series = jnp.einsum("tc,fcn->ftn", table, row_block, precision=highest)
    base_east, base_north, step_east, step_north = (series[0], series[1], series[2], series[3])
    magnitude = jnp.sqrt(base_east * base_east + base_north * base_north + SPEED_SOFT)
    projected = (base_east * step_east + base_north * step_north) / magnitude
    force_east = drag_row * (magnitude * step_east + base_east * projected)
    force_north = drag_row * (magnitude * step_north + base_north * projected)
    forces = jnp.stack([force_east, force_north])
    analysed = jnp.einsum("tc,ftn->fcn", table, forces, precision=highest) * (2.0 / table.shape[0])
    drag_rate = drag_row * jnp.mean(magnitude, axis=0)
    return (analysed, drag_rate)


def precondition(residual, angular, rotation, drag_rate):
    shaped = residual.reshape((3, residual.shape[1] // 2, 2) + residual.shape[2:])
    cos_part = shaped[:, :, 0]
    sin_part = shaped[:, :, 1]
    height_cos = -sin_part[0] / angular
    height_sin = cos_part[0] / angular
    real_rate = drag_rate + LINEAR_DRAG
    det_real = real_rate * real_rate - angular * angular + rotation * rotation
    det_imag = 2.0 * real_rate * angular
    det_norm = det_real * det_real + det_imag * det_imag
    inv_real = det_real / det_norm
    inv_imag = -det_imag / det_norm
    east_re = cos_part[1]
    east_im = -sin_part[1]
    north_re = cos_part[2]
    north_im = -sin_part[2]
    num_east_re = real_rate * east_re - angular * east_im + rotation * north_re
    num_east_im = real_rate * east_im + angular * east_re + rotation * north_im
    num_north_re = -rotation * east_re + real_rate * north_re - angular * north_im
    num_north_im = -rotation * east_im + real_rate * north_im + angular * north_re
    east_out_re = num_east_re * inv_real - num_east_im * inv_imag
    east_out_im = num_east_re * inv_imag + num_east_im * inv_real
    north_out_re = num_north_re * inv_real - num_north_im * inv_imag
    north_out_im = num_north_re * inv_imag + num_north_im * inv_real
    cosines = jnp.stack([height_cos, east_out_re, north_out_re])
    sines = jnp.stack([height_sin, -east_out_im, -north_out_im])
    return jnp.stack([cosines, sines], axis=2).reshape(residual.shape)


def local(direction, base_flow, water_depth, drag_factor, wet_mask):
    local_coefs = direction.shape[1]
    tile_rows = direction.shape[2]
    tile_cols = direction.shape[3]
    groups = lax.axis_size("freq")
    member = lax.axis_index("freq")
    band_rows = tile_rows // groups
    lat_place = lax.axis_index("lat")
    lat_count = lax.axis_size("lat")
    total_rows = tile_rows * lat_count
    wet_cells = wet_mask.astype(jnp.float32)
    height = direction[0] * wet_cells
    east = direction[1] * wet_cells
    north = direction[2] * wet_cells
    planes = jnp.stack([height, east, north, water_depth * east, water_depth * north])
    extended = extended_2(planes, (("lat", 2), ("lon", 3)), 1)
    rim_keep = jnp.ones((tile_rows + 2,), jnp.float32)
    rim_keep = rim_keep.at[0].set(jnp.where(lat_place == 0, 0.0, 1.0))
    rim_keep = rim_keep.at[tile_rows + 1].set(jnp.where(lat_place == lat_count - 1, 0.0, 1.0))
    extended = extended * rim_keep[:, None]
    local_count = local_coefs // 2
    first_con = member * local_count
    angular_local = OMEGA_STEP * (first_con + jnp.arange(local_count, dtype=jnp.int32) + 1).astype(
        jnp.float32
    )
    row_global = lat_place * tile_rows + jnp.arange(tile_rows, dtype=jnp.int32)
    rotation = rotation_of(row_global, total_rows)
    linear_part = linear_residual(
        extended, tile_rows, tile_cols, angular_local[:, None, None], rotation[:, None]
    )
    table = samples_table(NTIME, NCON)
    flows = jnp.concatenate([base_flow, jnp.stack([east, north])], axis=0)
    band_start = member * band_rows
    drag_band = lax.dynamic_slice_in_dim(drag_factor, band_start, band_rows, 0)
    flows_band, linear_band = (
        lax.all_to_all(flows, "freq", split_axis=2, concat_axis=1, tiled=True),
        lax.all_to_all(linear_part, "freq", split_axis=2, concat_axis=1, tiled=True),
    )
    mask_band = lax.dynamic_slice_in_dim(wet_cells, band_start, band_rows, 0)
    rotation_band = rotation_of(
        lat_place * tile_rows + band_start + jnp.arange(band_rows, dtype=jnp.int32), total_rows
    )
    angular_all = OMEGA_STEP * jnp.arange(1, NCON + 1, dtype=jnp.float32)

    def finish_row(items):
        row_block, linear_row, drag_row, mask_row, rotation_row = items
        friction, drag_rate = friction_row(row_block, drag_row, table)
        residual = (
            linear_row + jnp.concatenate([jnp.zeros_like(friction[:1]), friction], axis=0)
        ) * mask_row
        return precondition(residual, angular_all[:, None], rotation_row, drag_rate)

    band_result = lax.map(
        finish_row,
        (
            jnp.moveaxis(flows_band, 2, 0),
            jnp.moveaxis(linear_band, 2, 0),
            drag_band,
            mask_band,
            rotation_band,
        ),
    )
    band_result = jnp.moveaxis(band_result, 0, 2)
    return lax.all_to_all(band_result, "freq", split_axis=1, concat_axis=2, tiled=True)


def solution(mesh):
    placed = (
        P(None, "freq", "lat", "lon"),
        P(None, "freq", "lat", "lon"),
        P("lat", "lon"),
        P("lat", "lon"),
        P("lat", "lon"),
    )
    return jax.shard_map(
        local, mesh=mesh, in_specs=placed, out_specs=P(None, "freq", "lat", "lon"), check_vma=False
    )
```

profile of v0, /device:TPU:8, one launch (start us, length us, event | category | flops | bytes accessed | tf_op | source)
XLA Modules:
  0.0 540.2 jit_solution(4843827294149295579)
XLA Ops:
  8.5 2.4 collective-permute-start
  10.9 3.4 collective-permute-start.1
  26.3 5.9 %maximum_multiply_fusion = f32[5,4,130,514]{3,2,1,0:T(8,128)S(1)} fusion(f32[5,4,130,1]{3,2,1,0:T(8,128)S(1)} %copy.113, f32[5,4,1,512]{3,2,1,0:T(1,128)S(1)} %copy.109, f32[5,4,128,512]{3,2,1,0:T(8,128)} %copy-done, f32[5,4,1,512]{3,2,1,0:T(1,128)S(1)} %copy.108, f32[5,4,130,1]{3,2,1,0:T(8,128)S(1)} %copy.112, f32[130]{0:T(256)S(1)} %constant_dynamic-update-slice_fusion.2), kind=kLoop, calls=%fused_computation.57 | loop fusion | flops 6682000 | bytes 10691720 | tf_op jit(solution)/shard_map/mul | solution.py:150
  35.2 2.7 fusion.27
  38.2 3.7 copy.114
  41.9 8.5 %all-to-all-start = ((f32[3,4,128,512]{3,1,0,2:T(4,128)}), f32[3,4,128,512]{3,1,0,2:T(4,128)S(1)}, u32[]{:S(2)}, u32[]{:S(2)}) async-start(f32[3,4,128,512]{3,1,0,2:T(4,128)} %copy.114), calls=%async_computation | async-start | bytes 6291456 | tf_op jit(solution)/shard_map/all_to_all | solution.py:167
  55.7 2.7 pad_maximum_fusion.1
  58.3 66.8 %all-to-all-done = f32[3,4,128,512]{3,1,0,2:T(4,128)S(1)} async-done(((f32[3,4,128,512]{3,1,0,2:T(4,128)}), f32[3,4,128,512]{3,1,0,2:T(4,128)S(1)}, u32[]{:S(2)}, u32[]{:S(2)}) %all-to-all-start) | async-done | bytes 3145760 | tf_op jit(solution)/shard_map/all_to_all | solution.py:167
  125.1 4.6 all-to-all-start.1
  130.7 2.7 copy.115
  133.4 4.9 all_to_all.42
  138.3 88.1 %all-to-all-done.1 = f32[4,4,128,512]{3,1,0,2:T(4,128)} async-done(((f32[4,4,128,512]{3,1,0,2:T(4,128)}), f32[4,4,128,512]{3,1,0,2:T(4,128)}, u32[]{:S(2)}, u32[]{:S(2)}) %all-to-all-start.1) | async-done | bytes 4194336 | tf_op jit(solution)/shard_map/all_to_all | solution.py:166
  226.5 5.4 %copy.119 = f32[4,8,4,16,512]{4,2,1,0,3:T(4,128)} copy(f32[4,8,4,16,512]{4,2,0,3,1:T(4,128)} %bitcast.12) | data formatting | bytes 8388608 | tf_op jit(solution)/shard_map/all_to_all | solution.py:166
  231.9 5.3 all_to_all.46
  237.2 225.5 %while.15 = (s32[]{:T(128)}, f32[16,3,32,512]{3,0,1,2:T(8,128)}, f32[16,3,32,512]{3,2,1,0:T(8,128)}, f32[16,512]{1,0:T(8,128)S(1)}, f32[16,4,32,512]{3,2,1,0:T(8...) while((s32[]{:T(128)}, f32[16,3,32,512]{3,0,1,2:T(8,128)}, ...), condition=%wide.region_2.3_spmd.clone.clone, body=%wide.region_0.0_spmd.clone.clone.sunk | while | flops 305752128 | bytes 11770913 | solution.py:183
  237.2 2.9 convolution_bitcast_fusion.2
  246.3 5.0 dynamic_update_slice.8
  251.2 2.9 convolution_bitcast_fusion.2
  260.4 5.0 dynamic_update_slice.8
  265.3 2.9 convolution_bitcast_fusion.2
  274.5 5.0 dynamic_update_slice.8
  279.4 2.9 convolution_bitcast_fusion.2
  288.6 5.0 dynamic_update_slice.8
  293.5 2.9 convolution_bitcast_fusion.2
  302.7 5.0 dynamic_update_slice.8
  307.6 2.9 convolution_bitcast_fusion.2
  316.8 5.0 dynamic_update_slice.8
  321.7 2.9 convolution_bitcast_fusion.2
  330.9 5.0 dynamic_update_slice.8
  335.8 2.9 convolution_bitcast_fusion.2
  344.9 5.0 dynamic_update_slice.8
  349.9 2.9 convolution_bitcast_fusion.2
  359.0 5.0 dynamic_update_slice.8
  364.0 2.9 convolution_bitcast_fusion.2
  373.1 5.0 dynamic_update_slice.8
  378.1 2.9 convolution_bitcast_fusion.2
  387.2 5.0 dynamic_update_slice.8
  392.2 2.9 convolution_bitcast_fusion.2
  401.3 5.0 dynamic_update_slice.8
  406.3 2.9 convolution_bitcast_fusion.2
  415.4 5.0 dynamic_update_slice.8
  420.4 2.9 convolution_bitcast_fusion.2
  429.5 5.0 dynamic_update_slice.8
  434.5 2.9 convolution_bitcast_fusion.2
  443.6 5.0 dynamic_update_slice.8
  448.6 2.9 convolution_bitcast_fusion.2
  457.7 5.0 dynamic_update_slice.8
  462.7 75.6 %all_to_all.54 = f32[3,32,16,512]{3,2,0,1:T(8,128)S(1)} all-to-all(f32[3,32,16,512]{3,2,0,1:T(8,128)} %bitcast.160), channel_id=1, replica_groups=mesh['freq'=8,'lat'=8,'lon'=4] {'freq'}, dimensions={1} | all-to-all | bytes 6291456 | tf_op jit(solution)/shard_map/all_to_all | solution.py:194
  (360 shorter events, 102.5 us)
Async XLA Ops:
  2.3 3.4 copy-start.4
  3.9 2.2 copy-start.1
  5.7 2.7 copy-start.2
  6.0 2.4 copy-start
  8.5 8.0 %collective-permute-start = (f32[5,4,1,512]{3,0,2,1:T(8,128)S(1)}, f32[5,4,1,512]{3,0,2,1:T(8,128)S(1)}, u32[]{:S(2)}, u32[]{:S(2)}) collective-permute-start(f32[5,4,1,512]{3,0,2,1:T(8,128)S(1)} %copy.106), channel_id=1, source_target_pairs={{0,4},{4,8},{8,12},{12,16},{16,20},{20,24},{24,28},{28,0},{1,5},{5... | collective-permute-start | bytes 122888 | tf_op jit(solution)/shard_map/ppermute | solution.py:24
  10.9 6.5 %collective-permute-start.1 = (f32[5,4,1,512]{3,0,2,1:T(8,128)S(1)}, f32[5,4,1,512]{3,0,2,1:T(8,128)S(1)}, u32[]{:S(2)}, u32[]{:S(2)}) collective-permute-start(f32[5,4,1,512]{3,0,2,1:T(8,128)S(1)} %copy.107), channel_id=1, source_target_pairs={{4,0},{8,4},{12,8},{16,12},{20,16},{24,20},{28,24},{0,28},{5,1},{9... | collective-permute-start | bytes 122888 | tf_op jit(solution)/shard_map/ppermute | solution.py:27
  21.0 3.4 collective-permute-start.2
  22.2 3.6 collective-permute-start.3
  41.9 83.2 %all-to-all-start = ((f32[3,4,128,512]{3,1,0,2:T(4,128)}), f32[3,4,128,512]{3,1,0,2:T(4,128)S(1)}, u32[]{:S(2)}, u32[]{:S(2)}) async-start(f32[3,4,128,512]{3,1,0,2:T(4,128)} %copy.114), calls=%async_computation | async-start | bytes 6291456 | tf_op jit(solution)/shard_map/all_to_all | solution.py:167
  50.3 4.0 copy-start.3
  125.1 101.4 %all-to-all-start.1 = ((f32[4,4,128,512]{3,1,0,2:T(4,128)}), f32[4,4,128,512]{3,1,0,2:T(4,128)}, u32[]{:S(2)}, u32[]{:S(2)}) async-start(f32[4,4,128,512]{3,1,0,2:T(4,128)} %pad_maximum_fusion.1), calls=%async_computation.1 | async-start | bytes 8388608 | tf_op jit(solution)/shard_map/all_to_all | solution.py:166
where the time goes:
time: 544 us; the launch traced here: 540 us
  waiting for transfers between devices  159 us (29%)
  local copies, waits for them, and re-layouts  136 us (25%)
  blocking collectives  75.6 us (14%)
  other arithmetic  61.9 us (11%)
  matrix products  57.8 us (11%)
  loops' own time  29.1 us (5%)
  starting transfers between devices  20.8 us (4%)
    all_to_all x1, waiting for transfers between devices, local(): lax.all_to_all(flows, 'freq', split_axis=2, concat_axis=1, tiled=True)  88.1 us
    dynamic_update_slice x48, local copies, waits for them, and re-layouts, local(): lax.map(finish_row, (jnp.moveaxis(flows_band, 2, 0), jnp.moveaxis(linear_...  86.2 us
    all_to_all x1, blocking collectives, local(): lax.all_to_all(band_result, 'freq', split_axis=1, concat_axis=2, tiled=True)  75.6 us
    all_to_all x1, waiting for transfers between devices, local(): lax.all_to_all(linear_part, 'freq', split_axis=2, concat_axis=1, tiled=True)  66.8 us
    dot_general x16, matrix products, friction_row(): series = jnp.einsum('tc,fcn->ftn', table, row_block, precision=highest)  46.1 us
    another operation x1, loops' own time, local(): lax.map(finish_row, (jnp.moveaxis(flows_band, 2, 0), jnp.moveaxis(linear_...  29.1 us
    mul x16, other arithmetic, finish_row(): (linear_row + jnp.concatenate([jnp.zeros_like(friction[:1]), friction], a...  15.4 us
    dot_general x16, matrix products, friction_row(): jnp.einsum('tc,ftn->fcn', table, forces, precision=highest)  11.7 us
  transfers between devices with their start and end apart: 6, of which 6 were waited for; matrix products, arithmetic and copies ran while one was open for 2% of the time, Pallas kernels for 0%

commit v1 on v0

--- a/solution.py
+++ b/solution.py
@@ -128,6 +128,23 @@
     return jnp.stack([cosines, sines], axis=2).reshape(residual.shape)
 
 
+def friction_band(flows_band, drag_band, table):
+    highest = lax.Precision.HIGHEST
+    fields, coefs, rows, cols = flows_band.shape
+    block = flows_band.reshape(fields, coefs, rows * cols)
+    series = jnp.einsum("tc,fcn->ftn", table, block, precision=highest)
+    base_east, base_north, step_east, step_north = (series[0], series[1], series[2], series[3])
+    drag_row = drag_band.reshape(1, rows * cols)
+    magnitude = jnp.sqrt(base_east * base_east + base_north * base_north + SPEED_SOFT)
+    projected = (base_east * step_east + base_north * step_north) / magnitude
+    force_east = drag_row * (magnitude * step_east + base_east * projected)
+    force_north = drag_row * (magnitude * step_north + base_north * projected)
+    forces = jnp.stack([force_east, force_north])
+    analysed = jnp.einsum("tc,ftn->fcn", table, forces, precision=highest) * (2.0 / table.shape[0])
+    drag_rate = drag_row[0] * lax.optimization_barrier(jnp.mean(magnitude, axis=0))
+    return analysed.reshape(2, coefs, rows, cols), drag_rate.reshape(rows, cols)
+
+
 def local(direction, base_flow, water_depth, drag_factor, wet_mask):
     local_coefs = direction.shape[1]
     tile_rows = direction.shape[2]
@@ -142,6 +159,8 @@
     height = direction[0] * wet_cells
     east = direction[1] * wet_cells
     north = direction[2] * wet_cells
+    flows = jnp.concatenate([base_flow, jnp.stack([east, north])], axis=0)
+    flows_band = lax.all_to_all(flows, "freq", split_axis=2, concat_axis=1, tiled=True)
     planes = jnp.stack([height, east, north, water_depth * east, water_depth * north])
     extended = extended_2(planes, (("lat", 2), ("lon", 3)), 1)
     rim_keep = jnp.ones((tile_rows + 2,), jnp.float32)
@@ -159,39 +178,15 @@
         extended, tile_rows, tile_cols, angular_local[:, None, None], rotation[:, None]
     )
     table = samples_table(NTIME, NCON)
-    flows = jnp.concatenate([base_flow, jnp.stack([east, north])], axis=0)
     band_start = member * band_rows
     drag_band = lax.dynamic_slice_in_dim(drag_factor, band_start, band_rows, 0)
-    flows_band, linear_band = (
-        lax.all_to_all(flows, "freq", split_axis=2, concat_axis=1, tiled=True),
-        lax.all_to_all(linear_part, "freq", split_axis=2, concat_axis=1, tiled=True),
-    )
-    mask_band = lax.dynamic_slice_in_dim(wet_cells, band_start, band_rows, 0)
-    rotation_band = rotation_of(
-        lat_place * tile_rows + band_start + jnp.arange(band_rows, dtype=jnp.int32), total_rows
-    )
-    angular_all = OMEGA_STEP * jnp.arange(1, NCON + 1, dtype=jnp.float32)
-
-    def finish_row(items):
-        row_block, linear_row, drag_row, mask_row, rotation_row = items
-        friction, drag_rate = friction_row(row_block, drag_row, table)
-        residual = (
-            linear_row + jnp.concatenate([jnp.zeros_like(friction[:1]), friction], axis=0)
-        ) * mask_row
-        return precondition(residual, angular_all[:, None], rotation_row, drag_rate)
-
-    band_result = lax.map(
-        finish_row,
-        (
-            jnp.moveaxis(flows_band, 2, 0),
-            jnp.moveaxis(linear_band, 2, 0),
-            drag_band,
-            mask_band,
-            rotation_band,
-        ),
-    )
-    band_result = jnp.moveaxis(band_result, 0, 2)
-    return lax.all_to_all(band_result, "freq", split_axis=1, concat_axis=2, tiled=True)
+    analysed_band, drag_rate_band = friction_band(flows_band, drag_band, table)
+    friction = lax.all_to_all(analysed_band, "freq", split_axis=1, concat_axis=2, tiled=True)
+    drag_rate = lax.all_gather(drag_rate_band, "freq", axis=0, tiled=True)
+    residual = (
+        linear_part + jnp.concatenate([jnp.zeros_like(friction[:1]), friction], axis=0)
+    ) * wet_cells
+    return precondition(residual, angular_local[:, None, None], rotation[:, None], drag_rate)
 
 
 def solution(mesh):

time: 544 us -> 298 us (0.55)
  local copies, waits for them, and re-layouts: 136 us -> 30.6 us
  waiting for transfers between devices: 159 us -> 95.9 us
  blocking collectives: 75.6 us -> 32 us
  loops' own time: 29.1 us -> 0 us
  other arithmetic: 61.9 us -> 53.1 us
    dynamic_update_slice x48 -> x0, local copies, waits for them, and re-layouts: 86.2 us -> none  [local(): lax.map(finish_row, (jnp.moveaxis(flows_band, 2, 0), jnp.moveaxis(linear_...]
    all_to_all x1 -> x0, blocking collectives: 75.6 us -> none  [local(): lax.all_to_all(band_result, 'freq', split_axis=1, concat_axis=2, tiled=True)]
    all_to_all x1, waiting for transfers between devices: 66.8 us -> 0.01 us  [local(): lax.all_to_all(analysed_band, 'freq', split_axis=1, concat_axis=2, tiled=...]
    all_gather x0 -> x1, blocking collectives: none -> 32 us  [local(): drag_rate = lax.all_gather(drag_rate_band, 'freq', axis=0, tiled=True)]
    another operation x1 -> x0, loops' own time: 29.1 us -> none  [local(): lax.map(finish_row, (jnp.moveaxis(flows_band, 2, 0), jnp.moveaxis(linear_...]
    sub x16 -> x1, other arithmetic: 10.7 us -> 0.77 us  [precondition(): east_out_re = num_east_re * inv_real - num_east_im * inv_imag]
    dynamic_slice x17 -> x0, local copies, waits for them, and re-layouts: 9.76 us -> none  [the longest x16 8.99 us: local(): lax.map(finish_row, (jnp.moveaxis(flows_band, 2, 0), jnp.moveaxis(linear_...]
    all_to_all x3 -> x1, local copies, waits for them, and re-layouts: 9.57 us -> 0.17 us  [local(): lax.all_to_all(analysed_band, 'freq', split_axis=1, concat_axis=2, tiled=...]
  transfers between devices with their start and end apart: 6 -> 6, of which waited for: 6 -> 3; matrix products, arithmetic and copies ran while one was open for 2% -> 10% of each run, Pallas kernels for 0% -> 0%
where the time goes in v1:
time: 298 us; the launch traced here: 294 us
  waiting for transfers between devices  95.9 us (32%)
  matrix products  61.4 us (21%)
  other arithmetic  53.1 us (18%)
  blocking collectives  32 us (11%)
  local copies, waits for them, and re-layouts  30.6 us (10%)
  starting transfers between devices  20.5 us (7%)
    all_to_all x1, waiting for transfers between devices, local(): lax.all_to_all(flows, 'freq', split_axis=2, concat_axis=1, tiled=True)  93.7 us
    dot_general x1, matrix products, friction_band(): series = jnp.einsum('tc,fcn->ftn', table, block, precision=highest)  47.7 us
    all_gather x1, blocking collectives, local(): drag_rate = lax.all_gather(drag_rate_band, 'freq', axis=0, tiled=True)  32 us
    mul x1, other arithmetic, friction_band(): force_east = drag_row * (magnitude * step_east + base_east * projected)  18.2 us
    dot_general x1, matrix products, friction_band(): jnp.einsum('tc,ftn->fcn', table, forces, precision=highest)  13.7 us
    all_to_all x1, starting transfers between devices, local(): lax.all_to_all(flows, 'freq', split_axis=2, concat_axis=1, tiled=True)  9.18 us
    unnamed x4, other arithmetic  8.68 us
    all_to_all x1, local copies, waits for them, and re-layouts, local(): lax.all_to_all(flows, 'freq', split_axis=2, concat_axis=1, tiled=True)  6.64 us
  transfers between devices with their start and end apart: 6, of which 3 were waited for; matrix products, arithmetic and copies ran while one was open for 10% of the time, Pallas kernels for 0%

profile of v1, /device:TPU:8, one launch (start us, length us, event | category | flops | bytes accessed | tf_op | source)
XLA Modules:
  0.0 294.1 jit_solution(5827438192637905519)
XLA Ops:
  0.0 1.0 convert_element_type.48
  1.0 2.4 multiply_dynamic-update-slice_fusion.2
  3.4 2.5 constant_dynamic-update-slice_fusion.1
  5.9 2.7 constant_dynamic-update-slice_fusion
  8.5 0.7 copy.89
  9.2 0.7 copy.88
  9.9 1.4 copy.87
  11.3 2.7 pad_maximum_fusion
  13.9 9.2 %all-to-all-start = ((f32[4,4,128,512]{3,1,0,2:T(4,128)}), f32[4,4,128,512]{3,1,0,2:T(4,128)}, u32[]{:S(2)}, u32[]{:S(2)}) async-start(f32[4,4,128,512]{3,1,0,2:T(4,128)} %pad_maximum_fusion), calls=%async_computation | async-start | bytes 8388608 | tf_op jit(solution)/shard_map/all_to_all | solution.py:163
  23.1 0.2 fusion.33
  23.4 1.2 multiply_dynamic-update-slice_fusion.1
  24.6 1.2 multiply_dynamic-update-slice_fusion
  25.8 93.7 %all-to-all-done = f32[4,4,128,512]{3,1,0,2:T(4,128)} async-done(((f32[4,4,128,512]{3,1,0,2:T(4,128)}), f32[4,4,128,512]{3,1,0,2:T(4,128)}, u32[]{:S(2)}, u32[]{:S(2)}) %all-to-all-start) | async-done | bytes 4194336 | tf_op jit(solution)/shard_map/all_to_all | solution.py:163
  119.4 6.6 %copy.110 = f32[4,4,8,16,512]{4,3,1,2,0:T(8,128)} copy(f32[4,4,8,16,512]{4,1,0,3,2:T(4,128)} %bitcast.8) | data formatting | bytes 8388608 | tf_op jit(solution)/shard_map/all_to_all | solution.py:163
  126.1 5.0 %reshape.520 = f32[4,32,8192]{2,1,0:T(8,128)} reshape(f32[4,8,4,16,512]{4,3,2,1,0:T(8,128)} %bitcast.142) | data formatting | bytes 8388608 | tf_op jit(solution)/shard_map/reshape | solution.py:134
  131.1 47.7 %convolution_bitcast_fusion = f32[4,256,8192]{2,1,0:T(8,128)} fusion(f32[4,32,8192]{2,1,0:T(8,128)} %reshape.520, f32[256,32,1]{0,1,2:T(8,128)S(1)} %reshape.526), kind=kOutput, calls=%fused_computation | convolution fusion | flops 3221225472 | bytes 37781504 | tf_op jit(solution)/shard_map/tc,fcn->ftn/dot_general | solution.py:135
  178.8 18.2 %add_multiply_fusion.1 = (f32[1,256,8192]{2,1,0:T(8,128)}, f32[1,256,8192]{2,1,0:T(8,128)}, f32[8192]{0:T(1024)S(1)}) fusion(f32[4,256,8192]{2,1,0:T(8,128)} %convolution_bitcast_fusion, f32[8192]{0:T(1024)S(1)} %bitcast.154), kind=kLoop, calls=%fused_computation.7 | loop fusion | flops 35643392 | bytes 50397184 | tf_op jit(solution)/shard_map/mul | solution.py:140
  197.0 13.7 %fusion.4 = f32[2,8192,32]{1,2,0:T(8,128)S(1)} fusion(f32[256,32,1]{0,1,2:T(8,128)S(1)} %reshape.526, f32[1,256,8192]{2,1,0:T(8,128)} %get-tuple-element.40, f32[1,256,8192]{2,1,0:T(8,128)} %get-tuple-element.39), kind=kOutput, calls=%fused_computation.5 | convolution fusion | flops 1615331328 | bytes 18907136 | tf_op jit(solution)/shard_map/tc,ftn->fcn/dot_general | solution.py:143
  210.7 1.2 copy.108
  211.9 1.6 copy.92
  213.5 3.6 %all-to-all-start.1 = ((f32[2,32,16,512]{3,2,0,1:T(8,128)}), f32[2,32,16,512]{3,2,0,1:T(8,128)S(1)}, u32[]{:S(2)}, u32[]{:S(2)}) async-start(f32[2,32,16,512]{3,2,0,1:T(8,128)} %copy.92), calls=%async_computation.1 | async-start | bytes 4194304 | tf_op jit(solution)/shard_map/all_to_all | solution.py:184
  217.1 1.1 fusion.40
  218.3 2.4 collective-permute-start
  220.6 3.5 %collective-permute-start.1 = (f32[5,4,1,512]{3,2,1,0:T(1,128)S(1)}, f32[5,4,1,512]{3,2,1,0:T(1,128)S(1)}, u32[]{:S(2)}, u32[]{:S(2)}) collective-permute-start(f32[5,4,1,512]{3,2,1,0:T(1,128)S(1)} %get-tuple-element.50), channel_id=1, source_target_pairs={{4,0},{8,4},{12,8},{16,12},{20,16},{24,20},{28,24},{0,28},{5,1},{9... | collective-permute-start | bytes 122888 | tf_op jit(solution)/shard_map/ppermute | solution.py:27
  224.2 1.8 collective-permute-done
  226.0 0.4 collective-permute-done.1
  226.4 3.8 %pad_maximum_fusion.4 = (f32[5,4,130,1]{3,2,1,0:T(8,128)}, f32[5,4,130,1]{3,2,1,0:T(8,128)}) fusion(f32[5,4,1,512]{3,2,1,0:T(1,128)S(1)} %collective-permute-done.1, f32[5,4,128,512]{3,2,1,0:T(8,128)} %multiply_dynamic-update-slice_fusion, f32[5,4,1,512]{3,2,1,0:T(1,128)S(1)} %collective-permute-done), kind=kLoop, calls=%fused_computation.22 | loop fusion | flops 10400 | bytes 5345600 | tf_op jit(solution)/shard_map/slice | solution.py:25
  230.2 2.5 copy.83
  232.8 2.6 copy.84
  235.3 1.8 collective-permute-start.3
  237.2 1.6 copy.85
  238.8 1.6 copy.86
  240.4 6.2 %maximum_multiply_fusion = f32[5,4,130,514]{3,2,1,0:T(8,128)S(1)} fusion(f32[5,4,130,1]{3,2,1,0:T(8,128)} %copy.86, f32[5,4,1,512]{3,2,1,0:T(1,128)S(1)} %collective-permute-done.1, f32[5,4,128,512]{3,2,1,0:T(8,128)} %multiply_dynamic-update-slice_fusion, f32[5,4,1,512]{3,2,1,0:T(1,128)S(1)} %collective-permute-done, f32[5,4,130,1]{3,2,1,0:T(8,128)} %copy.85, ...), kind=kLoop, calls=%fused_computation.12 | loop fusion | flops 6682000 | bytes 10691720 | tf_op jit(solution)/shard_map/mul | solution.py:169
  246.6 0.4 slice.187
  247.0 0.2 slice_multiply_fusion.8
  247.3 2.7 slice_subtract_fusion.2
  250.0 0.4 slice_multiply_fusion.4
  250.5 3.9 %fusion.12 = (f32[1,4,128,512]{3,2,1,0:T(8,128)}, f32[1,4,128,512]{3,2,1,0:T(8,128)}) fusion(f32[5,4,130,514]{3,2,1,0:T(8,128)S(1)} %maximum_multiply_fusion, f32[128]{0:T(128)S(1)} %broadcast_multiply_fusion.2, f32[1,4,128,512]{3,2,1,0:T(8,128)S(1)} %bitcast.151, f32[1,4,128,512]{3,2,1,0:T(8,128)S(1)} %bitcast.150), kind=kLoop, calls=%fused_computation.31 | loop fusion | flops 4718592 | bytes 15729152 | tf_op jit(solution)/shard_map/add | solution.py:74
  254.5 32.0 %all_gather.3 = f32[128,512]{1,0:T(8,128)S(1)} all-gather(f32[16,512]{1,0:T(8,128)S(1)} %reshape.524), channel_id=1, replica_groups=mesh['freq'=8,'lat'=8,'lon'=4] {'freq'}, dimensions={0}, use_global_device_ids=true | all-gather | bytes 294912 | tf_op jit(solution)/shard_map/all_gather | solution.py:185
  286.6 0.2 copy.94
  286.7 1.0 copy-done.2
  287.8 0.3 copy-done.3
  288.1 1.9 fusion.8
  290.0 0.8 multiply_subtract_fusion.2
  290.9 0.4 add_negate_fusion.1
  291.3 0.1 maximum_bitcast_fusion.1
  291.5 0.3 pad_maximum_fusion.1
  291.8 2.0 copy.100
  (35 shorter events, 0.7 us)
Async XLA Ops:
  0.0 23.4 %copy-start = (f32[128,512]{1,0:T(8,128)S(1)}, f32[128,512]{1,0:T(8,128)}, u32[]{:S(2)}) copy-start(f32[128,512]{1,0:T(8,128)} %param.12) | copy-start | bytes 786436
  5.9 4.0 %copy-start.4 = (f32[2,4,128,512]{3,2,1,0:T(8,128)S(1)}, f32[2,4,128,512]{3,2,1,0:T(8,128)}, u32[]{:S(2)}) copy-start(f32[2,4,128,512]{3,2,1,0:T(8,128)} %param.10) | copy-start | bytes 6291460
  13.9 9.5 %copy-start.5 = (f32[128,512]{1,0:T(8,128)S(1)}, f32[128,512]{1,0:T(8,128)}, u32[]{:S(2)}) copy-start(f32[128,512]{1,0:T(8,128)} %param.11) | copy-start | bytes 786436
  13.9 105.5 %all-to-all-start = ((f32[4,4,128,512]{3,1,0,2:T(4,128)}), f32[4,4,128,512]{3,1,0,2:T(4,128)}, u32[]{:S(2)}, u32[]{:S(2)}) async-start(f32[4,4,128,512]{3,1,0,2:T(4,128)} %pad_maximum_fusion), calls=%async_computation | async-start | bytes 8388608 | tf_op jit(solution)/shard_map/all_to_all | solution.py:163
  213.5 73.0 %all-to-all-start.1 = ((f32[2,32,16,512]{3,2,0,1:T(8,128)}), f32[2,32,16,512]{3,2,0,1:T(8,128)S(1)}, u32[]{:S(2)}, u32[]{:S(2)}) async-start(f32[2,32,16,512]{3,2,0,1:T(8,128)} %copy.92), calls=%async_computation.1 | async-start | bytes 4194304 | tf_op jit(solution)/shard_map/all_to_all | solution.py:184
  218.3 7.7 %collective-permute-start = (f32[5,4,1,512]{3,2,1,0:T(1,128)S(1)}, f32[5,4,1,512]{3,2,1,0:T(1,128)S(1)}, u32[]{:S(2)}, u32[]{:S(2)}) collective-permute-start(f32[5,4,1,512]{3,2,1,0:T(1,128)S(1)} %get-tuple-element.49), channel_id=1, source_target_pairs={{0,4},{4,8},{8,12},{12,16},{16,20},{20,24},{24,28},{28,0},{1,5},{5... | collective-permute-start | bytes 122888 | tf_op jit(solution)/shard_map/ppermute | solution.py:24
  220.6 5.8 %collective-permute-start.1 = (f32[5,4,1,512]{3,2,1,0:T(1,128)S(1)}, f32[5,4,1,512]{3,2,1,0:T(1,128)S(1)}, u32[]{:S(2)}, u32[]{:S(2)}) collective-permute-start(f32[5,4,1,512]{3,2,1,0:T(1,128)S(1)} %get-tuple-element.50), channel_id=1, source_target_pairs={{4,0},{8,4},{12,8},{16,12},{20,16},{24,20},{28,24},{0,28},{5,1},{9... | collective-permute-start | bytes 122888 | tf_op jit(solution)/shard_map/ppermute | solution.py:27
  232.7 4.4 %collective-permute-start.2 = (f32[5,4,130,1]{2,0,3,1:T(8,128)S(1)}, f32[5,4,130,1]{2,0,3,1:T(8,128)S(1)}, u32[]{:S(2)}, u32[]{:S(2)}) collective-permute-start(f32[5,4,130,1]{2,0,3,1:T(8,128)S(1)} %copy.83), channel_id=1, source_target_pairs={{0,1},{1,2},{2,3},{3,0},{4,5},{5,6},{6,7},{7,4},{8,9},{9,10},{10,1... | collective-permute-start | bytes 31208 | tf_op jit(solution)/shard_map/ppermute | solution.py:24
  235.3 3.4 %collective-permute-start.3 = (f32[5,4,130,1]{2,0,3,1:T(8,128)S(1)}, f32[5,4,130,1]{2,0,3,1:T(8,128)S(1)}, u32[]{:S(2)}, u32[]{:S(2)}) collective-permute-start(f32[5,4,130,1]{2,0,3,1:T(8,128)S(1)} %copy.84), channel_id=1, source_target_pairs={{1,0},{2,1},{3,2},{0,3},{5,4},{6,5},{7,6},{4,7},{9,8},{10,9},{11,1... | collective-permute-start | bytes 31208 | tf_op jit(solution)/shard_map/ppermute | solution.py:27
  286.5 1.2 copy-start.2
  286.5 1.5 copy-start.3
  291.5 2.3 copy-start.1
